TPU v7x, 256 devices: a whole 4x4x8 slice. The times are simulated.
256 devices in a mesh: walk: 64 (over z, x, core), elec: 2 (over y_lo), chol: 2 (over y_hi).
Axes of the slice: x: 4, y: 4 (y_hi: 2, y_lo: 2; y = y_hi * 2 + y_lo), z: 8, core: 2. Of those that a mesh axis runs over, the one named last changes fastest.
Arguments:
- green: bfloat16 [64, 1024, 256], P('walk'), may hold values from -6 to 6
- chol_vecs: bfloat16 [128, 256, 1024], P(('walk', 'chol'), 'elec'), may hold values from -0.1875 to 0.1875
Outputs:
- gradient: float32 [64, 1024, 256], P('walk', ('elec', 'chol'))
All inputs are finite; a program needn't handle non-finite values.
Results may differ from a plain program's by a relative error of at most 0.0029.
Values may be sent and summed in bfloat16 or wider, within the bound.
No kernel may reach another device: no remote copies, remote signals or barrier semaphores. Data moves between devices by JAX's collectives and lax.ppermute only.
A program may use at most 64 MiB of HBM per device.

v0:
```python
import functools

import jax
import jax.numpy as jnp
from jax import lax
from jax.experimental import pallas as pl
from jax.experimental.pallas import tpu as pltpu
from jax.sharding import Mesh, PartitionSpec as P


STEPS = [
    {"d": ("e", "e"), "b": ("e", "e"), "c": ("e", "e"), "a": ("e", "e")},
    {"b": ("a", "e"), "a": ("b", "e"), "d": ("e", "c"), "c": ("b", "e")},
    {"a": ("e", "c"), "d": ("a", "e"), "c": ("ba", "e"), "b": ("e", "d")},
    {"b": ("e", "cd"), "c": ("ab", "e"), "a": ("ab", "e"), "d": ("ab", "e")},
    {"c": ("a", "d"), "b": ("ba", "c"), "a": ("b", "d"), "d": ("ba", "c")},
    {"c": ("ab", "d"), "b": ("aba", "e"), "d": ("aba", "e"), "a": ("ab", "c")},
    {"b": ("ba", "d"), "a": ("bab", "c"), "c": ("bab", "c"), "d": ("bab", "c")},
    {"c": ("aba", "d"), "b": ("aba", "d"), "d": ("abab", "c")},
]


def along_z(word, letter):
    if word == "e":
        return letter
    if word == "abab":
        return {"b": "aba", "a": "bab"}[letter]
    if word[-1] == letter:
        return word[:-1] or "e"
    return "abab" if word + letter == "baba" else word + letter


def along_x(word, letter):
    if word == "e":
        return letter
    if word == letter:
        return "e"
    if word == "cd":
        return "d" if letter == "c" else "c"
    return "cd"


def moved(label, letter):
    if letter in "ab":
        return along_z(label[0], letter), label[1]
    return label[0], along_x(label[1], letter)


def pairs(n, odd):
    return [(i, ((i - odd) ^ 1) + odd if odd <= i < n - odd else n - 1 - i) for i in range(n)]


def exchanged(value, letter, sizes):
    axis = "z" if letter in "ab" else "x"
    return lax.ppermute(value, axis, pairs(sizes[axis], int(letter in "bd")))


VMEM = pl.BlockSpec(memory_space=pltpu.VMEM)
SMEM = pl.BlockSpec(memory_space=pltpu.SMEM)
PIECES = (((2, 0), (1, 0), (3, 1), (1, 1)), ((0, 0), (3, 0), (0, 1), (2, 1)))


def absorb(count, first, last, here_ref, own_ref, other_ref, *refs):
    halves = refs[: 2 * count]
    start_ref = None if first else refs[2 * count]
    outs = refs[2 * count + (0 if first else 1) :]
    electrons = own_ref.shape[1]
    half = electrons // 2
    width = own_ref.shape[0] // 4
    lefts = []
    for green in (own_ref, other_ref):
        inter = [
            jnp.dot(h[...], green[...], preferred_element_type=jnp.float32).astype(jnp.bfloat16)
            for h in halves
        ]
        lefts.append(
            jnp.concatenate(
                [jnp.concatenate(inter[2 * m : 2 * m + 2], axis=0) for m in range(count)], axis=1
            )
        )
    left = jnp.concatenate(lefts, axis=0)
    here = here_ref[0]
    for r in range(4):
        columns = pl.ds(pl.multiple_of(lax.bitwise_xor(here, r) * width, width), width)
        right = jnp.concatenate([h[:, columns] for h in halves], axis=0)
        part = jnp.dot(left, right, preferred_element_type=jnp.float32)
        value = -part if first else start_ref[r] - part
        if not last:
            outs[0][r] = value
            continue
        for group, pieces in enumerate(PIECES):
            for at, (chunk, low) in enumerate(pieces):
                if chunk == r:
                    rows = slice(low * half, (low + 1) * half)
                    outs[group][at] = value[:electrons][rows]
                    outs[2 + group][at] = value[electrons:][rows]


def absorbed(here, own, other, halves, total, last):
    count = len(halves) // 2
    orbitals, electrons = own.shape
    first = total is None
    operands = [here, own, other, *halves] + ([] if first else [total])
    if last:
        shape = [jax.ShapeDtypeStruct((4, electrons // 2, orbitals // 4), jnp.float32)] * 4
    else:
        shape = jax.ShapeDtypeStruct((4, 2 * electrons, orbitals // 4), jnp.float32)
    flops = 2 * 2 * count * 2 * electrons * electrons * orbitals
    return pl.pallas_call(
        functools.partial(absorb, count, first, last),
        out_shape=shape,
        in_specs=[SMEM] + [VMEM] * (len(operands) - 1),
        out_specs=[VMEM] * 4 if last else VMEM,
        input_output_aliases={} if first or last else {len(operands) - 1: 0},
        cost_estimate=pl.CostEstimate(flops=flops, bytes_accessed=4 << 20, transcendentals=0),
        compiler_params=pltpu.CompilerParams(vmem_limit_bytes=VLIM << 20),
    )(*operands)


def finish(odd_ref, a_ref, b_ref, a_far_ref, b_far_ref, out_ref):
    half = a_ref.shape[0]
    for place, near, far in ((0, a_ref, a_far_ref), (1, b_ref, b_far_ref)):
        columns = pl.ds(pl.multiple_of(lax.bitwise_xor(odd_ref[0], place) * half, half), half)
        out_ref[:, columns] = (near[...] + far[...]).T


def lag(core_ref, block_ref, out_ref, work_ref):
    del block_ref, out_ref

    @pl.when(core_ref[0] == 1)
    def _():
        work_ref[...] = jnp.zeros_like(work_ref)

        @pl.loop(0, LAG)
        def _(i):
            work_ref[...] = work_ref[...] * 0.5 + 1.0


def lagged(core, block):
    return pl.pallas_call(
        lag,
        out_shape=jax.ShapeDtypeStruct(block.shape, block.dtype),
        in_specs=[SMEM, pl.BlockSpec(memory_space=pl.ANY)],
        out_specs=pl.BlockSpec(memory_space=pl.ANY),
        scratch_shapes=[pltpu.VMEM((8, 128), jnp.float32)],
        input_output_aliases={1: 0},
        compiler_params=pltpu.CompilerParams(vmem_limit_bytes=1 << 20),
    )(core, block)


LAG = 0
VLIM = 8


def shards_in(sizes, green, chol_vecs):
    odd = lax.rem(lax.axis_index("x"), 2)
    own = green[0]
    electrons = own.shape[1]
    half = electrons // 2
    here = (lax.axis_index("elec") * 2 + lax.axis_index("chol")).reshape(1)

    def to_core(v):
        return lax.ppermute(v, "core", [(0, 1), (1, 0)])

    def to_e(v):
        return lax.ppermute(v, "elec", [(0, 1), (1, 0)])

    def to_o(v):
        return lax.ppermute(v, ("elec", "chol"), [(0, 3), (3, 0), (1, 2), (2, 1)])

    cycle = []
    for x in range(0, sizes["x"], 2):
        ring = [(x, 0), (x + 1, 0), (x + 1, 1), (x, 1)]
        at = [i * 2 + e for i, e in ring]
        cycle += [(at[i], at[(i + 1) % 4]) for i in range(4)]
    first = lax.ppermute(chol_vecs[0], ("x", "elec"), cycle)
    if LAG:
        first = lagged(lax.axis_index("core").reshape(1), first)
    own = jnp.where(odd == 1, jnp.roll(own, half, axis=1), own)
    other = to_core(own)
    first, other = lax.optimization_barrier((first, other))

    held = {("e", "e"): first}
    total = None
    done = set()
    for number, step in enumerate(STEPS):
        new = {}
        for s, label in step.items():
            new[moved(label, s)] = exchanged(held[label], s, sizes)
        held.update(new)
        ready = []
        for z in sorted({label[0] for label in held}):
            for one, two in (("c", "e"), ("d", "cd")):
                if (z, one) in held and (z, two) in held and (z, one) not in done:
                    done.add((z, one))
                    ready += [held[z, one], held[z, two]]
        if ready:
            total = absorbed(here, own, other, ready, total, number == len(STEPS) - 1)

    keep_1, keep_2, give_1, give_2 = total
    sum_1 = keep_1 + to_core(give_1)
    sum_2 = keep_2 + to_core(give_2)
    a, b = to_e(sum_1[:2]), to_o(sum_1[2:])
    a_far = to_o(sum_2[1] + a[1])
    b_far = to_e(sum_2[3] + b[1])
    out = pl.pallas_call(
        finish,
        out_shape=jax.ShapeDtypeStruct((green.shape[1] // 4, electrons), jnp.float32),
        in_specs=[SMEM] + [VMEM] * 4,
        out_specs=VMEM,
        compiler_params=pltpu.CompilerParams(vmem_limit_bytes=4 << 20),
    )(odd.reshape(1), sum_2[0] + a[0], sum_2[2] + b[0], a_far, b_far)
    return out[None]


def solution(mesh):
    sizes = {"z": 8, "x": 4, "core": 2, "elec": 2, "chol": 2}
    fine = Mesh(mesh.devices.reshape(tuple(sizes.values())), tuple(sizes))
    walk = ("z", "x", "core")
    in_specs = (P(walk, None, None), P((*walk, "chol"), "elec", None))
    out_specs = P(walk, ("elec", "chol"), None)
    return jax.shard_map(
        functools.partial(shards_in, sizes), mesh=fine, in_specs=in_specs, out_specs=out_specs, check_vma=False
    )
```

profile of v0, /device:TPU:1, one launch (start us, length us, event | category | flops | bytes accessed | tf_op | source)
XLA Modules:
  0.0 108.8 jit_solution(16799975205297326119)
XLA Ops:
  1.1 1.2 %maximum_select_fusion.own_ref = bf16[1024,256]{1,0:T(8,128)(2,1)S(1)} fusion(bf16[1024,128]{1,0:T(8,128)(2,1)S(1)} %get-tuple-element.26, bf16[1024,128]{1,0:T(8,128)(2,1)S(1)} %get-tuple-element.25, pred[]{:T(512)S(6)} %eq.3, bf16[1,1024,256]{2,1,0:T(8,128)(2,1)} %param.2), kind=kLoop, calls=%fused_computation | loop fusion | flops 1310720 | bytes 1572865 | tf_op jit(solution)/shard_map/jit(_where)/select_n | solution.py:179
  2.3 3.3 %collective-permute-start.1 = (bf16[1024,256]{1,0:T(8,128)(2,1)S(1)}, bf16[1024,256]{1,0:T(8,128)(2,1)S(1)}, u32[]{:S(2)}, u32[]{:S(2)}) collective-permute-start(bf16[1024,256]{1,0:T(8,128)(2,1)S(1)} %maximum_select_fusion.own_ref), channel_id=1, source_target_pairs={{0,4},{4,0},{1,5},{5,1},{2,6},{6,2},{3,7},{7,3},{8,12},{12,8},{9,1... | collective-permute-start | bytes 1572872 | tf_op jit(solution)/shard_map/ppermute | solution.py:163
  5.6 7.8 %collective-permute-done.refs_1_ = bf16[128,1024]{1,0:T(8,128)(2,1)S(1)} collective-permute-done((bf16[128,1024]{1,0:T(8,128)(2,1)S(1)}, bf16[128,1024]{1,0:T(8,128)(2,1)S(1)}, u32[]{:S(2)}, u32[]{:S(2)}) %collective-permute-start) | collective-permute-done | bytes 262176 | tf_op jit(solution)/shard_map/ppermute | solution.py:176
  13.6 4.8 %collective-permute-start.8 = (bf16[128,1024]{1,0:T(8,128)(2,1)S(1)}, bf16[128,1024]{1,0:T(8,128)(2,1)S(1)}, u32[]{:S(2)}, u32[]{:S(2)}) collective-permute-start(bf16[128,1024]{1,0:T(8,128)(2,1)S(1)} %collective-permute-done.refs_1_), channel_id=1, source_target_pairs={{0,224},{32,64},{64,32},{96,128},{128,96},{160,192},{192,160},{224... | collective-permute-start | bytes 786440 | tf_op jit(solution)/shard_map/ppermute | solution.py:55
  18.4 1.8 %collective-permute-start.16 = (bf16[128,1024]{1,0:T(8,128)(2,1)S(1)}, bf16[128,1024]{1,0:T(8,128)(2,1)S(1)}, u32[]{:S(2)}, u32[]{:S(2)}) collective-permute-start(bf16[128,1024]{1,0:T(8,128)(2,1)S(1)} %collective-permute-done.refs_1_), channel_id=1, source_target_pairs={{0,24},{8,16},{16,8},{24,0},{1,25},{9,17},{17,9},{25,1},{2,26},{10... | collective-permute-start | bytes 786440 | tf_op jit(solution)/shard_map/ppermute | solution.py:55
  21.8 2.0 %collective-permute-done.8.refs_1_ = bf16[128,1024]{1,0:T(8,128)(2,1)S(1)} collective-permute-done((bf16[128,1024]{1,0:T(8,128)(2,1)S(1)}, bf16[128,1024]{1,0:T(8,128)(2,1)S(1)}, u32[]{:S(2)}, u32[]{:S(2)}) %collective-permute-start.8) | collective-permute-done | bytes 262176 | tf_op jit(solution)/shard_map/ppermute | solution.py:55
  24.8 2.6 %collective-permute-start.3 = (bf16[128,1024]{1,0:T(8,128)(2,1)S(1)}, bf16[128,1024]{1,0:T(8,128)(2,1)S(1)}, u32[]{:S(2)}, u32[]{:S(2)}) collective-permute-start(bf16[128,1024]{1,0:T(8,128)(2,1)S(1)} %collective-permute-done.2.refs_1_), channel_id=1, source_target_pairs={{0,224},{32,64},{64,32},{96,128},{128,96},{160,192},{192,160},{224... | collective-permute-start | bytes 786440 | tf_op jit(solution)/shard_map/ppermute | solution.py:55
  28.1 3.6 %collective-permute-done.29.refs_3_ = bf16[128,1024]{1,0:T(8,128)(2,1)S(1)} collective-permute-done((bf16[128,1024]{1,0:T(8,128)(2,1)S(1)}, bf16[128,1024]{1,0:T(8,128)(2,1)S(1)}, u32[]{:S(2)}, u32[]{:S(2)}) %collective-permute-start.29) | collective-permute-done | bytes 262176 | tf_op jit(solution)/shard_map/ppermute | solution.py:55
  31.6 2.1 %collective-permute-start.17 = (bf16[128,1024]{1,0:T(8,128)(2,1)S(1)}, bf16[128,1024]{1,0:T(8,128)(2,1)S(1)}, u32[]{:S(2)}, u32[]{:S(2)}) collective-permute-start(bf16[128,1024]{1,0:T(8,128)(2,1)S(1)} %collective-permute-done.16.refs_2_), channel_id=1, source_target_pairs={{0,224},{32,64},{64,32},{96,128},{128,96},{160,192},{192,160},{224... | collective-permute-start | bytes 786440 | tf_op jit(solution)/shard_map/ppermute | solution.py:55
  33.7 1.6 %collective-permute-start.25 = (bf16[128,1024]{1,0:T(8,128)(2,1)S(1)}, bf16[128,1024]{1,0:T(8,128)(2,1)S(1)}, u32[]{:S(2)}, u32[]{:S(2)}) collective-permute-start(bf16[128,1024]{1,0:T(8,128)(2,1)S(1)} %collective-permute-done.2.refs_1_), channel_id=1, source_target_pairs={{0,24},{8,16},{16,8},{24,0},{1,25},{9,17},{17,9},{25,1},{2,26},{10... | collective-permute-start | bytes 786440 | tf_op jit(solution)/shard_map/ppermute | solution.py:55
  35.3 1.5 %collective-permute-start.23 = (bf16[128,1024]{1,0:T(8,128)(2,1)S(1)}, bf16[128,1024]{1,0:T(8,128)(2,1)}, u32[]{:S(2)}, u32[]{:S(2)}) collective-permute-start(bf16[128,1024]{1,0:T(8,128)(2,1)S(1)} %collective-permute-done.3.refs_1_), channel_id=1, source_target_pairs={{0,8},{8,0},{16,24},{24,16},{1,9},{9,1},{17,25},{25,17},{2,10},{10... | collective-permute-start | bytes 786440 | tf_op jit(solution)/shard_map/ppermute | solution.py:55
  38.5 2.3 %collective-permute-start.21 = (bf16[128,1024]{1,0:T(8,128)(2,1)S(1)}, bf16[128,1024]{1,0:T(8,128)(2,1)}, u32[]{:S(2)}, u32[]{:S(2)}) collective-permute-start(bf16[128,1024]{1,0:T(8,128)(2,1)S(1)} %collective-permute-done.3.refs_1_), channel_id=1, source_target_pairs={{0,24},{8,16},{16,8},{24,0},{1,25},{9,17},{17,9},{25,1},{2,26},{10... | collective-permute-start | bytes 786440 | tf_op jit(solution)/shard_map/ppermute | solution.py:55
  41.1 5.3 %collective-permute-done.23.refs_0_ = bf16[128,1024]{1,0:T(8,128)(2,1)} collective-permute-done((bf16[128,1024]{1,0:T(8,128)(2,1)S(1)}, bf16[128,1024]{1,0:T(8,128)(2,1)}, u32[]{:S(2)}, u32[]{:S(2)}) %collective-permute-start.23) | collective-permute-done | bytes 262176 | tf_op jit(solution)/shard_map/ppermute | solution.py:55
  47.1 1.2 %collective-permute-start.27 = (bf16[128,1024]{1,0:T(8,128)(2,1)}, bf16[128,1024]{1,0:T(8,128)(2,1)}, u32[]{:S(2)}, u32[]{:S(2)}) collective-permute-start(bf16[128,1024]{1,0:T(8,128)(2,1)} %collective-permute-done.10.refs_2_), channel_id=1, source_target_pairs={{0,24},{8,16},{16,8},{24,0},{1,25},{9,17},{17,9},{25,1},{2,26},{10... | collective-permute-start | bytes 786440 | tf_op jit(solution)/shard_map/ppermute | solution.py:55
  48.4 3.6 %collective-permute-done.26.refs_1_ = bf16[128,1024]{1,0:T(8,128)(2,1)S(1)} collective-permute-done((bf16[128,1024]{1,0:T(8,128)(2,1)S(1)}, bf16[128,1024]{1,0:T(8,128)(2,1)S(1)}, u32[]{:S(2)}, u32[]{:S(2)}) %collective-permute-start.26) | collective-permute-done | bytes 262176 | tf_op jit(solution)/shard_map/ppermute | solution.py:55
  57.6 2.2 %collective-permute-start.19 = (bf16[128,1024]{1,0:T(8,128)(2,1)S(1)}, bf16[128,1024]{1,0:T(8,128)(2,1)S(1)}, u32[]{:S(2)}, u32[]{:S(2)}) collective-permute-start(bf16[128,1024]{1,0:T(8,128)(2,1)S(1)} %copy-done.3), channel_id=1, source_target_pairs={{0,224},{32,64},{64,32},{96,128},{128,96},{160,192},{192,160},{224... | collective-permute-start | bytes 786440 | tf_op jit(solution)/shard_map/ppermute | solution.py:55
  60.2 1.4 %shard_map.29.refs_4_ = f32[4,512,256]{2,1,0:T(8,128)S(1)} custom-call(s32[1]{0:T(128)} %bitcast.1.here_ref, bf16[1024,256]{1,0:T(8,128)(2,1)S(1)} %maximum_select_fusion.own_ref, bf16[1024,256]{1,0:T(8,128)(2,1)S(1)} %collective-permute-done.1.other_ref, bf16[128,1024]{1,0:T(8,128)(2,1)S(1)} %collective-permute-done.32.refs_0_, ...), custom_call_target="tpu_custom_call", output_to_operand_aliasing={{}: (7, {})} | custom-call | flops 1073741824 | bytes 4194304 | tf_op jit(solution)/shard_map/pallas_call | solution.py:109
  61.6 2.4 %shard_map.30.refs_4_ = f32[4,512,256]{2,1,0:T(8,128)S(1)} custom-call(s32[1]{0:T(128)} %bitcast.1.here_ref, bf16[1024,256]{1,0:T(8,128)(2,1)S(1)} %maximum_select_fusion.own_ref, bf16[1024,256]{1,0:T(8,128)(2,1)S(1)} %collective-permute-done.1.other_ref, bf16[128,1024]{1,0:T(8,128)(2,1)S(1)} %copy-done.1, ...), custom_call_target="tpu_custom_call", output_to_operand_aliasing={{}: (7, {})} | custom-call | flops 1073741824 | bytes 4194304 | tf_op jit(solution)/shard_map/pallas_call | solution.py:109
  64.1 1.5 %collective-permute-start.20 = (bf16[128,1024]{1,0:T(8,128)(2,1)}, bf16[128,1024]{1,0:T(8,128)(2,1)S(1)}, u32[]{:S(2)}, u32[]{:S(2)}) collective-permute-start(bf16[128,1024]{1,0:T(8,128)(2,1)} %collective-permute-done.11.refs_2_), channel_id=1, source_target_pairs={{0,24},{8,16},{16,8},{24,0},{1,25},{9,17},{17,9},{25,1},{2,26},{10... | collective-permute-start | bytes 786440 | tf_op jit(solution)/shard_map/ppermute | solution.py:55
  65.6 2.3 %shard_map.31.refs_4_ = f32[4,512,256]{2,1,0:T(8,128)S(1)} custom-call(s32[1]{0:T(128)} %bitcast.1.here_ref, bf16[1024,256]{1,0:T(8,128)(2,1)S(1)} %maximum_select_fusion.own_ref, bf16[1024,256]{1,0:T(8,128)(2,1)S(1)} %collective-permute-done.1.other_ref, bf16[128,1024]{1,0:T(8,128)(2,1)} %collective-permute-done.23.refs_0_, ...), custom_call_target="tpu_custom_call", output_to_operand_aliasing={{}: (7, {})} | custom-call | flops 1073741824 | bytes 4194304 | tf_op jit(solution)/shard_map/pallas_call | solution.py:109
  70.5 2.3 %shard_map.32.refs_4_ = f32[4,512,256]{2,1,0:T(8,128)S(1)} custom-call(s32[1]{0:T(128)} %bitcast.1.here_ref, bf16[1024,256]{1,0:T(8,128)(2,1)S(1)} %maximum_select_fusion.own_ref, bf16[1024,256]{1,0:T(8,128)(2,1)S(1)} %collective-permute-done.1.other_ref, bf16[128,1024]{1,0:T(8,128)(2,1)S(1)} %collective-permute-done.25.refs_0_, ...), custom_call_target="tpu_custom_call", output_to_operand_aliasing={{}: (7, {})} | custom-call | flops 1073741824 | bytes 4194304 | tf_op jit(solution)/shard_map/pallas_call | solution.py:109
  72.8 2.6 %shard_map.33.refs_6_ = f32[4,512,256]{2,1,0:T(8,128)S(1)} custom-call(s32[1]{0:T(128)} %bitcast.1.here_ref, bf16[1024,256]{1,0:T(8,128)(2,1)S(1)} %maximum_select_fusion.own_ref, bf16[1024,256]{1,0:T(8,128)(2,1)S(1)} %collective-permute-done.1.other_ref, bf16[128,1024]{1,0:T(8,128)(2,1)} %collective-permute-done.21.refs_0_, ...), custom_call_target="tpu_custom_call", output_to_operand_aliasing={{}: (7, {})} | custom-call | flops 1073741824 | bytes 4194304 | tf_op jit(solution)/shard_map/pallas_call | solution.py:109
  75.4 3.0 %shard_map.34.refs_4_ = f32[4,512,256]{2,1,0:T(8,128)S(1)} custom-call(s32[1]{0:T(128)} %bitcast.1.here_ref, bf16[1024,256]{1,0:T(8,128)(2,1)S(1)} %maximum_select_fusion.own_ref, bf16[1024,256]{1,0:T(8,128)(2,1)S(1)} %collective-permute-done.1.other_ref, bf16[128,1024]{1,0:T(8,128)(2,1)S(1)} %collective-permute-done.12.refs_0_, ...), custom_call_target="tpu_custom_call", output_to_operand_aliasing={{}: (9, {})} | custom-call | flops 1610612736 | bytes 4194304 | tf_op jit(solution)/shard_map/pallas_call | solution.py:109
  78.4 1.3 %shard_map.35 = (f32[4,128,256]{2,1,0:T(8,128)S(1)}, f32[4,128,256]{2,1,0:T(8,128)S(1)}, f32[4,128,256]{2,1,0:T(8,128)S(1)}, f32[4,128,256]{2,1,0:T(8,128)S(1)}) custom-call(s32[1]{0:T(128)} %bitcast.1.here_ref, bf16[1024,256]{1,0:T(8,128)(2,1)S(1)} %maximum_select_fusion.own_ref, bf16[1024,256]{1,0:T(8,128)(2,1)S(1)} %collective-permute-done.1.other_ref, ...), custom_call_target="tpu_custom_call" | custom-call | flops 1073741824 | bytes 4194304 | tf_op jit(solution)/shard_map/pallas_call | solution.py:109
  79.8 10.6 %collective-permute-start.34 = (f32[4,128,256]{2,1,0:T(8,128)S(1)}, f32[4,128,256]{2,1,0:T(8,128)S(1)}, u32[]{:S(2)}, u32[]{:S(2)}) collective-permute-start(f32[4,128,256]{2,1,0:T(8,128)S(1)} %get-tuple-element.16), channel_id=1, source_target_pairs={{0,4},{4,0},{1,5},{5,1},{2,6},{6,2},{3,7},{7,3},{8,12},{12,8},{9,1... | collective-permute-start | bytes 1572872 | tf_op jit(solution)/shard_map/ppermute | solution.py:163
  90.4 1.4 %collective-permute-done.34 = f32[4,128,256]{2,1,0:T(8,128)S(1)} collective-permute-done((f32[4,128,256]{2,1,0:T(8,128)S(1)}, f32[4,128,256]{2,1,0:T(8,128)S(1)}, u32[]{:S(2)}, u32[]{:S(2)}) %collective-permute-start.34) | collective-permute-done | bytes 524320 | tf_op jit(solution)/shard_map/ppermute | solution.py:163
  92.0 1.4 %collective-permute-start.35 = (f32[2,128,256]{2,1,0:T(8,128)S(1)}, f32[2,128,256]{2,1,0:T(8,128)S(1)}, u32[]{:S(2)}, u32[]{:S(2)}) collective-permute-start(f32[2,128,256]{2,1,0:T(8,128)S(1)} %get-tuple-element.24), channel_id=1, source_target_pairs={{0,2},{2,0},{1,3},{3,1},{4,6},{6,4},{5,7},{7,5},{8,10},{10,8},{9,1... | collective-permute-start | bytes 786440 | tf_op jit(solution)/shard_map/ppermute | solution.py:166
  93.4 1.9 %collective-permute-start.36 = (f32[2,128,256]{2,1,0:T(8,128)S(1)}, f32[2,128,256]{2,1,0:T(8,128)S(1)}, u32[]{:S(2)}, u32[]{:S(2)}) collective-permute-start(f32[2,128,256]{2,1,0:T(8,128)S(1)} %get-tuple-element.23), channel_id=1, source_target_pairs={{0,3},{3,0},{1,2},{2,1},{4,7},{7,4},{5,6},{6,5},{8,11},{11,8},{9,1... | collective-permute-start | bytes 786440 | tf_op jit(solution)/shard_map/ppermute | solution.py:169
  95.3 4.2 %collective-permute-done.35 = f32[2,128,256]{2,1,0:T(8,128)S(1)} collective-permute-done((f32[2,128,256]{2,1,0:T(8,128)S(1)}, f32[2,128,256]{2,1,0:T(8,128)S(1)}, u32[]{:S(2)}, u32[]{:S(2)}) %collective-permute-start.35) | collective-permute-done | bytes 262176 | tf_op jit(solution)/shard_map/ppermute | solution.py:166
  99.6 2.2 %collective-permute-done.36 = f32[2,128,256]{2,1,0:T(8,128)S(1)} collective-permute-done((f32[2,128,256]{2,1,0:T(8,128)S(1)}, f32[2,128,256]{2,1,0:T(8,128)S(1)}, u32[]{:S(2)}, u32[]{:S(2)}) %collective-permute-start.36) | collective-permute-done | bytes 262176 | tf_op jit(solution)/shard_map/ppermute | solution.py:169
  101.8 2.0 %collective-permute-start.37 = (f32[128,256]{1,0:T(8,128)S(1)}, f32[128,256]{1,0:T(8,128)S(1)}, u32[]{:S(2)}, u32[]{:S(2)}) collective-permute-start(f32[128,256]{1,0:T(8,128)S(1)} %get-tuple-element.22), channel_id=1, source_target_pairs={{0,3},{3,0},{1,2},{2,1},{4,7},{7,4},{5,6},{6,5},{8,11},{11,8},{9,1... | collective-permute-start | bytes 393224 | tf_op jit(solution)/shard_map/ppermute | solution.py:169
  103.8 3.1 %collective-permute-done.37.a_far_ref = f32[128,256]{1,0:T(8,128)S(1)} collective-permute-done((f32[128,256]{1,0:T(8,128)S(1)}, f32[128,256]{1,0:T(8,128)S(1)}, u32[]{:S(2)}, u32[]{:S(2)}) %collective-permute-start.37) | collective-permute-done | bytes 131104 | tf_op jit(solution)/shard_map/ppermute | solution.py:169
  (87 shorter events, 18.0 us)
Async XLA Ops:
  2.3 11.1 %collective-permute-start.1 = (bf16[1024,256]{1,0:T(8,128)(2,1)S(1)}, bf16[1024,256]{1,0:T(8,128)(2,1)S(1)}, u32[]{:S(2)}, u32[]{:S(2)}) collective-permute-start(bf16[1024,256]{1,0:T(8,128)(2,1)S(1)} %maximum_select_fusion.own_ref), channel_id=1, source_target_pairs={{0,4},{4,0},{1,5},{5,1},{2,6},{6,2},{3,7},{7,3},{8,12},{12,8},{9,1... | collective-permute-start | bytes 1572872 | tf_op jit(solution)/shard_map/ppermute | solution.py:163
  5.6 7.8 %collective-permute-start = (bf16[128,1024]{1,0:T(8,128)(2,1)S(1)}, bf16[128,1024]{1,0:T(8,128)(2,1)S(1)}, u32[]{:S(2)}, u32[]{:S(2)}) collective-permute-start(bf16[128,1024]{1,0:T(8,128)(2,1)S(1)} %bitcast.15), channel_id=1, source_target_pairs={{0,8},{8,10},{10,2},{2,0},{16,24},{24,26},{26,18},{18,16},{1,9},{9... | collective-permute-start | bytes 786440 | tf_op jit(solution)/shard_map/ppermute | solution.py:176
  13.4 7.6 %collective-permute-start.28 = (bf16[128,1024]{1,0:T(8,128)(2,1)S(1)}, bf16[128,1024]{1,0:T(8,128)(2,1)S(1)}, u32[]{:S(2)}, u32[]{:S(2)}) collective-permute-start(bf16[128,1024]{1,0:T(8,128)(2,1)S(1)} %collective-permute-done.refs_1_), channel_id=1, source_target_pairs={{0,8},{8,0},{16,24},{24,16},{1,9},{9,1},{17,25},{25,17},{2,10},{10... | collective-permute-start | bytes 786440 | tf_op jit(solution)/shard_map/ppermute | solution.py:55
  13.6 10.2 %collective-permute-start.8 = (bf16[128,1024]{1,0:T(8,128)(2,1)S(1)}, bf16[128,1024]{1,0:T(8,128)(2,1)S(1)}, u32[]{:S(2)}, u32[]{:S(2)}) collective-permute-start(bf16[128,1024]{1,0:T(8,128)(2,1)S(1)} %collective-permute-done.refs_1_), channel_id=1, source_target_pairs={{0,224},{32,64},{64,32},{96,128},{128,96},{160,192},{192,160},{224... | collective-permute-start | bytes 786440 | tf_op jit(solution)/shard_map/ppermute | solution.py:55
  18.4 8.9 %collective-permute-start.16 = (bf16[128,1024]{1,0:T(8,128)(2,1)S(1)}, bf16[128,1024]{1,0:T(8,128)(2,1)S(1)}, u32[]{:S(2)}, u32[]{:S(2)}) collective-permute-start(bf16[128,1024]{1,0:T(8,128)(2,1)S(1)} %collective-permute-done.refs_1_), channel_id=1, source_target_pairs={{0,24},{8,16},{16,8},{24,0},{1,25},{9,17},{17,9},{25,1},{2,26},{10... | collective-permute-start | bytes 786440 | tf_op jit(solution)/shard_map/ppermute | solution.py:55
  21.0 10.6 %collective-permute-start.29 = (bf16[128,1024]{1,0:T(8,128)(2,1)S(1)}, bf16[128,1024]{1,0:T(8,128)(2,1)S(1)}, u32[]{:S(2)}, u32[]{:S(2)}) collective-permute-start(bf16[128,1024]{1,0:T(8,128)(2,1)S(1)} %collective-permute-done.28.refs_0_), channel_id=1, source_target_pairs={{0,24},{8,16},{16,8},{24,0},{1,25},{9,17},{17,9},{25,1},{2,26},{10... | collective-permute-start | bytes 786440 | tf_op jit(solution)/shard_map/ppermute | solution.py:55
  23.9 9.8 %collective-permute-start.32 = (bf16[128,1024]{1,0:T(8,128)(2,1)S(1)}, bf16[128,1024]{1,0:T(8,128)(2,1)S(1)}, u32[]{:S(2)}, u32[]{:S(2)}) collective-permute-start(bf16[128,1024]{1,0:T(8,128)(2,1)S(1)} %collective-permute-done.8.refs_1_), channel_id=1, source_target_pairs={{0,8},{8,0},{16,24},{24,16},{1,9},{9,1},{17,25},{25,17},{2,10},{10... | collective-permute-start | bytes 786440 | tf_op jit(solution)/shard_map/ppermute | solution.py:55
  24.1 11.2 %collective-permute-start.9 = (bf16[128,1024]{1,0:T(8,128)(2,1)S(1)}, bf16[128,1024]{1,0:T(8,128)(2,1)S(1)}, u32[]{:S(2)}, u32[]{:S(2)}) collective-permute-start(bf16[128,1024]{1,0:T(8,128)(2,1)S(1)} %collective-permute-done.8.refs_1_), channel_id=1, source_target_pairs={{0,32},{32,0},{64,96},{96,64},{128,160},{160,128},{192,224},{224,1... | collective-permute-start | bytes 786440 | tf_op jit(solution)/shard_map/ppermute | solution.py:55
  24.8 10.5 %collective-permute-start.3 = (bf16[128,1024]{1,0:T(8,128)(2,1)S(1)}, bf16[128,1024]{1,0:T(8,128)(2,1)S(1)}, u32[]{:S(2)}, u32[]{:S(2)}) collective-permute-start(bf16[128,1024]{1,0:T(8,128)(2,1)S(1)} %collective-permute-done.2.refs_1_), channel_id=1, source_target_pairs={{0,224},{32,64},{64,32},{96,128},{128,96},{160,192},{192,160},{224... | collective-permute-start | bytes 786440 | tf_op jit(solution)/shard_map/ppermute | solution.py:55
  27.4 9.4 %collective-permute-start.31 = (bf16[128,1024]{1,0:T(8,128)(2,1)S(1)}, bf16[128,1024]{1,0:T(8,128)(2,1)S(1)}, u32[]{:S(2)}, u32[]{:S(2)}) collective-permute-start(bf16[128,1024]{1,0:T(8,128)(2,1)S(1)} %collective-permute-done.28.refs_0_), channel_id=1, source_target_pairs={{0,32},{32,0},{64,96},{96,64},{128,160},{160,128},{192,224},{224,1... | collective-permute-start | bytes 786440 | tf_op jit(solution)/shard_map/ppermute | solution.py:55
  33.7 7.2 %collective-permute-start.25 = (bf16[128,1024]{1,0:T(8,128)(2,1)S(1)}, bf16[128,1024]{1,0:T(8,128)(2,1)S(1)}, u32[]{:S(2)}, u32[]{:S(2)}) collective-permute-start(bf16[128,1024]{1,0:T(8,128)(2,1)S(1)} %collective-permute-done.2.refs_1_), channel_id=1, source_target_pairs={{0,24},{8,16},{16,8},{24,0},{1,25},{9,17},{17,9},{25,1},{2,26},{10... | collective-permute-start | bytes 786440 | tf_op jit(solution)/shard_map/ppermute | solution.py:55
  35.3 11.1 %collective-permute-start.23 = (bf16[128,1024]{1,0:T(8,128)(2,1)S(1)}, bf16[128,1024]{1,0:T(8,128)(2,1)}, u32[]{:S(2)}, u32[]{:S(2)}) collective-permute-start(bf16[128,1024]{1,0:T(8,128)(2,1)S(1)} %collective-permute-done.3.refs_1_), channel_id=1, source_target_pairs={{0,8},{8,0},{16,24},{24,16},{1,9},{9,1},{17,25},{25,17},{2,10},{10... | collective-permute-start | bytes 786440 | tf_op jit(solution)/shard_map/ppermute | solution.py:55
  37.5 8.9 %collective-permute-start.30 = (bf16[128,1024]{1,0:T(8,128)(2,1)S(1)}, bf16[128,1024]{1,0:T(8,128)(2,1)S(1)}, u32[]{:S(2)}, u32[]{:S(2)}) collective-permute-start(bf16[128,1024]{1,0:T(8,128)(2,1)S(1)} %collective-permute-done.29.refs_3_), channel_id=1, source_target_pairs={{0,224},{32,64},{64,32},{96,128},{128,96},{160,192},{192,160},{224... | collective-permute-start | bytes 786440 | tf_op jit(solution)/shard_map/ppermute | solution.py:55
  38.5 9.8 %collective-permute-start.21 = (bf16[128,1024]{1,0:T(8,128)(2,1)S(1)}, bf16[128,1024]{1,0:T(8,128)(2,1)}, u32[]{:S(2)}, u32[]{:S(2)}) collective-permute-start(bf16[128,1024]{1,0:T(8,128)(2,1)S(1)} %collective-permute-done.3.refs_1_), channel_id=1, source_target_pairs={{0,24},{8,16},{16,8},{24,0},{1,25},{9,17},{17,9},{25,1},{2,26},{10... | collective-permute-start | bytes 786440 | tf_op jit(solution)/shard_map/ppermute | solution.py:55
  40.8 7.5 %collective-permute-start.18 = (bf16[128,1024]{1,0:T(8,128)(2,1)S(1)}, bf16[128,1024]{1,0:T(8,128)(2,1)S(1)}, u32[]{:S(2)}, u32[]{:S(2)}) collective-permute-start(bf16[128,1024]{1,0:T(8,128)(2,1)S(1)} %collective-permute-done.17.refs_2_), channel_id=1, source_target_pairs={{0,32},{32,0},{64,96},{96,64},{128,160},{160,128},{192,224},{224,1... | collective-permute-start | bytes 786440 | tf_op jit(solution)/shard_map/ppermute | solution.py:55
  40.8 11.2 %collective-permute-start.26 = (bf16[128,1024]{1,0:T(8,128)(2,1)S(1)}, bf16[128,1024]{1,0:T(8,128)(2,1)S(1)}, u32[]{:S(2)}, u32[]{:S(2)}) collective-permute-start(bf16[128,1024]{1,0:T(8,128)(2,1)S(1)} %collective-permute-done.25.refs_0_), channel_id=1, source_target_pairs={{0,8},{8,0},{16,24},{24,16},{1,9},{9,1},{17,25},{25,17},{2,10},{10... | collective-permute-start | bytes 786440 | tf_op jit(solution)/shard_map/ppermute | solution.py:55
  47.1 10.1 %collective-permute-start.27 = (bf16[128,1024]{1,0:T(8,128)(2,1)}, bf16[128,1024]{1,0:T(8,128)(2,1)}, u32[]{:S(2)}, u32[]{:S(2)}) collective-permute-start(bf16[128,1024]{1,0:T(8,128)(2,1)} %collective-permute-done.10.refs_2_), channel_id=1, source_target_pairs={{0,24},{8,16},{16,8},{24,0},{1,25},{9,17},{17,9},{25,1},{2,26},{10... | collective-permute-start | bytes 786440 | tf_op jit(solution)/shard_map/ppermute | solution.py:55
  48.3 9.3 %collective-permute-start.22 = (bf16[128,1024]{1,0:T(8,128)(2,1)}, bf16[128,1024]{1,0:T(8,128)(2,1)}, u32[]{:S(2)}, u32[]{:S(2)}) collective-permute-start(bf16[128,1024]{1,0:T(8,128)(2,1)} %collective-permute-done.21.refs_0_), channel_id=1, source_target_pairs={{0,8},{8,0},{16,24},{24,16},{1,9},{9,1},{17,25},{25,17},{2,10},{10... | collective-permute-start | bytes 786440 | tf_op jit(solution)/shard_map/ppermute | solution.py:55
  48.3 11.5 %collective-permute-start.11 = (bf16[128,1024]{1,0:T(8,128)(2,1)}, bf16[128,1024]{1,0:T(8,128)(2,1)}, u32[]{:S(2)}, u32[]{:S(2)}) collective-permute-start(bf16[128,1024]{1,0:T(8,128)(2,1)} %collective-permute-done.10.refs_2_), channel_id=1, source_target_pairs={{0,224},{32,64},{64,32},{96,128},{128,96},{160,192},{192,160},{224... | collective-permute-start | bytes 786440 | tf_op jit(solution)/shard_map/ppermute | solution.py:55
  52.7 11.3 %collective-permute-start.24 = (bf16[128,1024]{1,0:T(8,128)(2,1)}, bf16[128,1024]{1,0:T(8,128)(2,1)}, u32[]{:S(2)}, u32[]{:S(2)}) collective-permute-start(bf16[128,1024]{1,0:T(8,128)(2,1)} %collective-permute-done.23.refs_0_), channel_id=1, source_target_pairs={{0,32},{32,0},{64,96},{96,64},{128,160},{160,128},{192,224},{224,1... | collective-permute-start | bytes 786440 | tf_op jit(solution)/shard_map/ppermute | solution.py:55
  53.4 10.7 %collective-permute-start.14 = (bf16[128,1024]{1,0:T(8,128)(2,1)}, bf16[128,1024]{1,0:T(8,128)(2,1)}, u32[]{:S(2)}, u32[]{:S(2)}) collective-permute-start(bf16[128,1024]{1,0:T(8,128)(2,1)} %collective-permute-done.4.refs_3_), channel_id=1, source_target_pairs={{0,224},{32,64},{64,32},{96,128},{128,96},{160,192},{192,160},{224... | collective-permute-start | bytes 786440 | tf_op jit(solution)/shard_map/ppermute | solution.py:55
  57.2 10.8 %collective-permute-start.5 = (bf16[128,1024]{1,0:T(8,128)(2,1)}, bf16[128,1024]{1,0:T(8,128)(2,1)S(1)}, u32[]{:S(2)}, u32[]{:S(2)}) collective-permute-start(bf16[128,1024]{1,0:T(8,128)(2,1)} %collective-permute-done.4.refs_3_), channel_id=1, source_target_pairs={{0,24},{8,16},{16,8},{24,0},{1,25},{9,17},{17,9},{25,1},{2,26},{10... | collective-permute-start | bytes 786440 | tf_op jit(solution)/shard_map/ppermute | solution.py:55
  57.6 11.2 %collective-permute-start.19 = (bf16[128,1024]{1,0:T(8,128)(2,1)S(1)}, bf16[128,1024]{1,0:T(8,128)(2,1)S(1)}, u32[]{:S(2)}, u32[]{:S(2)}) collective-permute-start(bf16[128,1024]{1,0:T(8,128)(2,1)S(1)} %copy-done.3), channel_id=1, source_target_pairs={{0,224},{32,64},{64,32},{96,128},{128,96},{160,192},{192,160},{224... | collective-permute-start | bytes 786440 | tf_op jit(solution)/shard_map/ppermute | solution.py:55
  59.8 10.0 %collective-permute-start.12 = (bf16[128,1024]{1,0:T(8,128)(2,1)}, bf16[128,1024]{1,0:T(8,128)(2,1)S(1)}, u32[]{:S(2)}, u32[]{:S(2)}) collective-permute-start(bf16[128,1024]{1,0:T(8,128)(2,1)} %collective-permute-done.11.refs_2_), channel_id=1, source_target_pairs={{0,32},{32,0},{64,96},{96,64},{128,160},{160,128},{192,224},{224,1... | collective-permute-start | bytes 786440 | tf_op jit(solution)/shard_map/ppermute | solution.py:55
  64.0 11.4 %collective-permute-start.15 = (bf16[128,1024]{1,0:T(8,128)(2,1)}, bf16[128,1024]{1,0:T(8,128)(2,1)S(1)}, u32[]{:S(2)}, u32[]{:S(2)}) collective-permute-start(bf16[128,1024]{1,0:T(8,128)(2,1)} %collective-permute-done.11.refs_2_), channel_id=1, source_target_pairs={{0,8},{8,0},{16,24},{24,16},{1,9},{9,1},{17,25},{25,17},{2,10},{10... | collective-permute-start | bytes 786440 | tf_op jit(solution)/shard_map/ppermute | solution.py:55
  64.1 11.3 %collective-permute-start.20 = (bf16[128,1024]{1,0:T(8,128)(2,1)}, bf16[128,1024]{1,0:T(8,128)(2,1)S(1)}, u32[]{:S(2)}, u32[]{:S(2)}) collective-permute-start(bf16[128,1024]{1,0:T(8,128)(2,1)} %collective-permute-done.11.refs_2_), channel_id=1, source_target_pairs={{0,24},{8,16},{16,8},{24,0},{1,25},{9,17},{17,9},{25,1},{2,26},{10... | collective-permute-start | bytes 786440 | tf_op jit(solution)/shard_map/ppermute | solution.py:55
  68.0 10.4 %collective-permute-start.6 = (bf16[128,1024]{1,0:T(8,128)(2,1)S(1)}, bf16[128,1024]{1,0:T(8,128)(2,1)S(1)}, u32[]{:S(2)}, u32[]{:S(2)}) collective-permute-start(bf16[128,1024]{1,0:T(8,128)(2,1)S(1)} %collective-permute-done.5.refs_0_), channel_id=1, source_target_pairs={{0,8},{8,0},{16,24},{24,16},{1,9},{9,1},{17,25},{25,17},{2,10},{10... | collective-permute-start | bytes 786440 | tf_op jit(solution)/shard_map/ppermute | solution.py:55
  68.8 9.6 %collective-permute-start.7 = (bf16[128,1024]{1,0:T(8,128)(2,1)S(1)}, bf16[128,1024]{1,0:T(8,128)(2,1)S(1)}, u32[]{:S(2)}, u32[]{:S(2)}) collective-permute-start(bf16[128,1024]{1,0:T(8,128)(2,1)S(1)} %collective-permute-done.5.refs_0_), channel_id=1, source_target_pairs={{0,224},{32,64},{64,32},{96,128},{128,96},{160,192},{192,160},{224... | collective-permute-start | bytes 786440 | tf_op jit(solution)/shard_map/ppermute | solution.py:55
  69.9 8.6 %collective-permute-start.13 = (bf16[128,1024]{1,0:T(8,128)(2,1)S(1)}, bf16[128,1024]{1,0:T(8,128)(2,1)S(1)}, u32[]{:S(2)}, u32[]{:S(2)}) collective-permute-start(bf16[128,1024]{1,0:T(8,128)(2,1)S(1)} %collective-permute-done.12.refs_0_), channel_id=1, source_target_pairs={{0,24},{8,16},{16,8},{24,0},{1,25},{9,17},{17,9},{25,1},{2,26},{10... | collective-permute-start | bytes 786440 | tf_op jit(solution)/shard_map/ppermute | solution.py:55
  79.8 12.1 %collective-permute-start.34 = (f32[4,128,256]{2,1,0:T(8,128)S(1)}, f32[4,128,256]{2,1,0:T(8,128)S(1)}, u32[]{:S(2)}, u32[]{:S(2)}) collective-permute-start(f32[4,128,256]{2,1,0:T(8,128)S(1)} %get-tuple-element.16), channel_id=1, source_target_pairs={{0,4},{4,0},{1,5},{5,1},{2,6},{6,2},{3,7},{7,3},{8,12},{12,8},{9,1... | collective-permute-start | bytes 1572872 | tf_op jit(solution)/shard_map/ppermute | solution.py:163
  92.0 7.6 %collective-permute-start.35 = (f32[2,128,256]{2,1,0:T(8,128)S(1)}, f32[2,128,256]{2,1,0:T(8,128)S(1)}, u32[]{:S(2)}, u32[]{:S(2)}) collective-permute-start(f32[2,128,256]{2,1,0:T(8,128)S(1)} %get-tuple-element.24), channel_id=1, source_target_pairs={{0,2},{2,0},{1,3},{3,1},{4,6},{6,4},{5,7},{7,5},{8,10},{10,8},{9,1... | collective-permute-start | bytes 786440 | tf_op jit(solution)/shard_map/ppermute | solution.py:166
  93.4 8.4 %collective-permute-start.36 = (f32[2,128,256]{2,1,0:T(8,128)S(1)}, f32[2,128,256]{2,1,0:T(8,128)S(1)}, u32[]{:S(2)}, u32[]{:S(2)}) collective-permute-start(f32[2,128,256]{2,1,0:T(8,128)S(1)} %get-tuple-element.23), channel_id=1, source_target_pairs={{0,3},{3,0},{1,2},{2,1},{4,7},{7,4},{5,6},{6,5},{8,11},{11,8},{9,1... | collective-permute-start | bytes 786440 | tf_op jit(solution)/shard_map/ppermute | solution.py:169
  (20 other events, 74.2 us)
where the time goes:
time: 111 us; the launch traced here: 109 us
  starting transfers between devices  47.6 us (43%)
  waiting for transfers between devices  35.9 us (32%)
  Pallas kernels  16.9 us (15%)
  local copies, waits for them, and re-layouts  6.61 us (6%)
  other arithmetic  1.39 us (1%)
    ppermute x31, starting transfers between devices, exchanged(): return lax.ppermute(value, axis, pairs(sizes[axis], int(letter in 'bd')))  28.4 us
    ppermute x31, waiting for transfers between devices, exchanged(): return lax.ppermute(value, axis, pairs(sizes[axis], int(letter in 'bd')))  16.2 us
    pallas_call x8, Pallas kernels, absorbed(): pl.pallas_call(functools.partial(absorb, count, first, last), out_shape=s...  16.1 us
    ppermute x3, starting transfers between devices, to_core(): return lax.ppermute(v, 'core', [(0, 1), (1, 0)])  14 us
    ppermute x1, waiting for transfers between devices, shards_in(): first = lax.ppermute(chol_vecs[0], ('x', 'elec'), cycle)  7.76 us
    unnamed x26, local copies, waits for them, and re-layouts  5.46 us
    ppermute x2, waiting for transfers between devices, to_o(): return lax.ppermute(v, ('elec', 'chol'), [(0, 3), (3, 0), (1, 2), (2, 1)])  5.35 us
    ppermute x2, waiting for transfers between devices, to_e(): return lax.ppermute(v, 'elec', [(0, 1), (1, 0)])  5.22 us
  transfers between devices with their start and end apart: 39, of which 13 were waited for; matrix products, arithmetic and copies ran while one was open for 0% of the time, Pallas kernels for 14%

commit v1 on v0

--- a/solution.py
+++ b/solution.py
@@ -200,9 +200,10 @@
     keep_1, keep_2, give_1, give_2 = total
     sum_1 = keep_1 + to_core(give_1)
     sum_2 = keep_2 + to_core(give_2)
-    a, b = to_e(sum_1[:2]), to_o(sum_1[2:])
-    a_far = to_o(sum_2[1] + a[1])
-    b_far = to_e(sum_2[3] + b[1])
+    near = sum_1.astype(jnp.bfloat16)
+    a, b = to_e(near[:2]), to_o(near[2:])
+    a_far = to_o((sum_2[1] + a[1]).astype(jnp.bfloat16))
+    b_far = to_e((sum_2[3] + b[1]).astype(jnp.bfloat16))
     out = pl.pallas_call(
         finish,
         out_shape=jax.ShapeDtypeStruct((green.shape[1] // 4, electrons), jnp.float32),

time: 111 us -> 107 us (0.964)
  the two profiles are of different devices: /device:TPU:1 before, /device:TPU:32 now
where the time goes in v1:
time: 107 us
  starting transfers between devices  50.5 us (47%)
  waiting for transfers between devices  31.1 us (29%)
  Pallas kernels  16.9 us (16%)
  local copies, waits for them, and re-layouts  6.59 us (6%)
  other arithmetic  1.38 us (1%)
    ppermute x31, starting transfers between devices, exchanged(): return lax.ppermute(value, axis, pairs(sizes[axis], int(letter in 'bd')))  42.2 us
    pallas_call x8, Pallas kernels, absorbed(): pl.pallas_call(functools.partial(absorb, count, first, last), out_shape=s...  16.1 us
    ppermute x31, waiting for transfers between devices, exchanged(): return lax.ppermute(value, axis, pairs(sizes[axis], int(letter in 'bd')))  14.1 us
    ppermute x1, waiting for transfers between devices, shards_in(): first = lax.ppermute(chol_vecs[0], ('x', 'elec'), cycle)  7.13 us
    ppermute x2, waiting for transfers between devices, to_o(): return lax.ppermute(v, ('elec', 'chol'), [(0, 3), (3, 0), (1, 2), (2, 1)])  5.77 us
    unnamed x26, local copies, waits for them, and re-layouts  5.47 us
    ppermute x2, starting transfers between devices, to_o(): return lax.ppermute(v, ('elec', 'chol'), [(0, 3), (3, 0), (1, 2), (2, 1)])  4.46 us
    ppermute x2, waiting for transfers between devices, to_e(): return lax.ppermute(v, 'elec', [(0, 1), (1, 0)])  2.7 us
  transfers between devices with their start and end apart: 39, of which 13 were waited for; matrix products, arithmetic and copies ran while one was open for 0% of the time, Pallas kernels for 14%

profile of v1, /device:TPU:32, one launch (start us, length us, event | category | flops | bytes accessed | tf_op | source)
XLA Modules:
  0.0 106.8 jit_solution(2177140451305732809)
XLA Ops:
  2.4 1.6 %collective-permute-start = (bf16[128,1024]{1,0:T(8,128)(2,1)S(1)}, bf16[128,1024]{1,0:T(8,128)(2,1)S(1)}, u32[]{:S(2)}, u32[]{:S(2)}) collective-permute-start(bf16[128,1024]{1,0:T(8,128)(2,1)S(1)} %bitcast.15), channel_id=1, source_target_pairs={{0,8},{8,10},{10,2},{2,0},{16,24},{24,26},{26,18},{18,16},{1,9},{9... | collective-permute-start | bytes 786440 | tf_op jit(solution)/shard_map/ppermute | solution.py:176
  4.0 7.1 %collective-permute-done.refs_1_ = bf16[128,1024]{1,0:T(8,128)(2,1)S(1)} collective-permute-done((bf16[128,1024]{1,0:T(8,128)(2,1)S(1)}, bf16[128,1024]{1,0:T(8,128)(2,1)S(1)}, u32[]{:S(2)}, u32[]{:S(2)}) %collective-permute-start) | collective-permute-done | bytes 262176 | tf_op jit(solution)/shard_map/ppermute | solution.py:176
  11.1 1.5 %collective-permute-start.28 = (bf16[128,1024]{1,0:T(8,128)(2,1)S(1)}, bf16[128,1024]{1,0:T(8,128)(2,1)S(1)}, u32[]{:S(2)}, u32[]{:S(2)}) collective-permute-start(bf16[128,1024]{1,0:T(8,128)(2,1)S(1)} %collective-permute-done.refs_1_), channel_id=1, source_target_pairs={{0,8},{8,0},{16,24},{24,16},{1,9},{9,1},{17,25},{25,17},{2,10},{10... | collective-permute-start | bytes 786440 | tf_op jit(solution)/shard_map/ppermute | solution.py:55
  12.6 1.9 %collective-permute-start.8 = (bf16[128,1024]{1,0:T(8,128)(2,1)S(1)}, bf16[128,1024]{1,0:T(8,128)(2,1)S(1)}, u32[]{:S(2)}, u32[]{:S(2)}) collective-permute-start(bf16[128,1024]{1,0:T(8,128)(2,1)S(1)} %collective-permute-done.refs_1_), channel_id=1, source_target_pairs={{0,224},{32,64},{64,32},{96,128},{128,96},{160,192},{192,160},{224... | collective-permute-start | bytes 786440 | tf_op jit(solution)/shard_map/ppermute | solution.py:55
  14.5 4.0 %collective-permute-start.2 = (bf16[128,1024]{1,0:T(8,128)(2,1)S(1)}, bf16[128,1024]{1,0:T(8,128)(2,1)S(1)}, u32[]{:S(2)}, u32[]{:S(2)}) collective-permute-start(bf16[128,1024]{1,0:T(8,128)(2,1)S(1)} %collective-permute-done.refs_1_), channel_id=1, source_target_pairs={{0,32},{32,0},{64,96},{96,64},{128,160},{160,128},{192,224},{224,1... | collective-permute-start | bytes 786440 | tf_op jit(solution)/shard_map/ppermute | solution.py:55
  18.6 2.1 %collective-permute-start.16 = (bf16[128,1024]{1,0:T(8,128)(2,1)S(1)}, bf16[128,1024]{1,0:T(8,128)(2,1)S(1)}, u32[]{:S(2)}, u32[]{:S(2)}) collective-permute-start(bf16[128,1024]{1,0:T(8,128)(2,1)S(1)} %collective-permute-done.refs_1_), channel_id=1, source_target_pairs={{0,24},{8,16},{16,8},{24,0},{1,25},{9,17},{17,9},{25,1},{2,26},{10... | collective-permute-start | bytes 786440 | tf_op jit(solution)/shard_map/ppermute | solution.py:55
  22.5 2.3 %collective-permute-start.9 = (bf16[128,1024]{1,0:T(8,128)(2,1)S(1)}, bf16[128,1024]{1,0:T(8,128)(2,1)S(1)}, u32[]{:S(2)}, u32[]{:S(2)}) collective-permute-start(bf16[128,1024]{1,0:T(8,128)(2,1)S(1)} %collective-permute-done.8.refs_1_), channel_id=1, source_target_pairs={{0,32},{32,0},{64,96},{96,64},{128,160},{160,128},{192,224},{224,1... | collective-permute-start | bytes 786440 | tf_op jit(solution)/shard_map/ppermute | solution.py:55
  25.9 3.1 %collective-permute-done.16.refs_2_ = bf16[128,1024]{1,0:T(8,128)(2,1)S(1)} collective-permute-done((bf16[128,1024]{1,0:T(8,128)(2,1)S(1)}, bf16[128,1024]{1,0:T(8,128)(2,1)S(1)}, u32[]{:S(2)}, u32[]{:S(2)}) %collective-permute-start.16) | collective-permute-done | bytes 262176 | tf_op jit(solution)/shard_map/ppermute | solution.py:55
  29.7 2.7 %collective-permute-done.29.refs_3_ = bf16[128,1024]{1,0:T(8,128)(2,1)S(1)} collective-permute-done((bf16[128,1024]{1,0:T(8,128)(2,1)S(1)}, bf16[128,1024]{1,0:T(8,128)(2,1)S(1)}, u32[]{:S(2)}, u32[]{:S(2)}) %collective-permute-start.29) | collective-permute-done | bytes 262176 | tf_op jit(solution)/shard_map/ppermute | solution.py:55
  33.3 2.1 %collective-permute-start.25 = (bf16[128,1024]{1,0:T(8,128)(2,1)S(1)}, bf16[128,1024]{1,0:T(8,128)(2,1)S(1)}, u32[]{:S(2)}, u32[]{:S(2)}) collective-permute-start(bf16[128,1024]{1,0:T(8,128)(2,1)S(1)} %collective-permute-done.2.refs_1_), channel_id=1, source_target_pairs={{0,24},{8,16},{16,8},{24,0},{1,25},{9,17},{17,9},{25,1},{2,26},{10... | collective-permute-start | bytes 786440 | tf_op jit(solution)/shard_map/ppermute | solution.py:55
  35.4 2.0 %collective-permute-start.23 = (bf16[128,1024]{1,0:T(8,128)(2,1)S(1)}, bf16[128,1024]{1,0:T(8,128)(2,1)}, u32[]{:S(2)}, u32[]{:S(2)}) collective-permute-start(bf16[128,1024]{1,0:T(8,128)(2,1)S(1)} %collective-permute-done.3.refs_1_), channel_id=1, source_target_pairs={{0,8},{8,0},{16,24},{24,16},{1,9},{9,1},{17,25},{25,17},{2,10},{10... | collective-permute-start | bytes 786440 | tf_op jit(solution)/shard_map/ppermute | solution.py:55
  39.9 2.4 %collective-permute-start.21 = (bf16[128,1024]{1,0:T(8,128)(2,1)S(1)}, bf16[128,1024]{1,0:T(8,128)(2,1)}, u32[]{:S(2)}, u32[]{:S(2)}) collective-permute-start(bf16[128,1024]{1,0:T(8,128)(2,1)S(1)} %collective-permute-done.3.refs_1_), channel_id=1, source_target_pairs={{0,24},{8,16},{16,8},{24,0},{1,25},{9,17},{17,9},{25,1},{2,26},{10... | collective-permute-start | bytes 786440 | tf_op jit(solution)/shard_map/ppermute | solution.py:55
  43.2 1.5 %collective-permute-done.10.refs_2_ = bf16[128,1024]{1,0:T(8,128)(2,1)} collective-permute-done((bf16[128,1024]{1,0:T(8,128)(2,1)S(1)}, bf16[128,1024]{1,0:T(8,128)(2,1)}, u32[]{:S(2)}, u32[]{:S(2)}) %collective-permute-start.10) | collective-permute-done | bytes 262176 | tf_op jit(solution)/shard_map/ppermute | solution.py:55
  44.7 4.8 %collective-permute-done.23.refs_0_ = bf16[128,1024]{1,0:T(8,128)(2,1)} collective-permute-done((bf16[128,1024]{1,0:T(8,128)(2,1)S(1)}, bf16[128,1024]{1,0:T(8,128)(2,1)}, u32[]{:S(2)}, u32[]{:S(2)}) %collective-permute-start.23) | collective-permute-done | bytes 262176 | tf_op jit(solution)/shard_map/ppermute | solution.py:55
  49.5 1.9 %collective-permute-start.4 = (bf16[128,1024]{1,0:T(8,128)(2,1)S(1)}, bf16[128,1024]{1,0:T(8,128)(2,1)}, u32[]{:S(2)}, u32[]{:S(2)}) collective-permute-start(bf16[128,1024]{1,0:T(8,128)(2,1)S(1)} %collective-permute-done.3.refs_1_), channel_id=1, source_target_pairs={{0,32},{32,0},{64,96},{96,64},{128,160},{160,128},{192,224},{224,1... | collective-permute-start | bytes 786440 | tf_op jit(solution)/shard_map/ppermute | solution.py:55
  55.1 2.3 %collective-permute-start.24 = (bf16[128,1024]{1,0:T(8,128)(2,1)}, bf16[128,1024]{1,0:T(8,128)(2,1)}, u32[]{:S(2)}, u32[]{:S(2)}) collective-permute-start(bf16[128,1024]{1,0:T(8,128)(2,1)} %collective-permute-done.23.refs_0_), channel_id=1, source_target_pairs={{0,32},{32,0},{64,96},{96,64},{128,160},{160,128},{192,224},{224,1... | collective-permute-start | bytes 786440 | tf_op jit(solution)/shard_map/ppermute | solution.py:55
  64.6 3.2 %collective-permute-start.12 = (bf16[128,1024]{1,0:T(8,128)(2,1)}, bf16[128,1024]{1,0:T(8,128)(2,1)S(1)}, u32[]{:S(2)}, u32[]{:S(2)}) collective-permute-start(bf16[128,1024]{1,0:T(8,128)(2,1)} %collective-permute-done.11.refs_2_), channel_id=1, source_target_pairs={{0,32},{32,0},{64,96},{96,64},{128,160},{160,128},{192,224},{224,1... | collective-permute-start | bytes 786440 | tf_op jit(solution)/shard_map/ppermute | solution.py:55
  67.8 1.4 %shard_map.29.refs_4_ = f32[4,512,256]{2,1,0:T(8,128)S(1)} custom-call(s32[1]{0:T(128)} %bitcast.1.here_ref, bf16[1024,256]{1,0:T(8,128)(2,1)S(1)} %maximum_select_fusion.own_ref, bf16[1024,256]{1,0:T(8,128)(2,1)S(1)} %collective-permute-done.1.other_ref, bf16[128,1024]{1,0:T(8,128)(2,1)S(1)} %collective-permute-done.32.refs_0_, ...), custom_call_target="tpu_custom_call", output_to_operand_aliasing={{}: (7, {})} | custom-call | flops 1073741824 | bytes 4194304 | tf_op jit(solution)/shard_map/pallas_call | solution.py:109
  69.2 2.4 %shard_map.30.refs_4_ = f32[4,512,256]{2,1,0:T(8,128)S(1)} custom-call(s32[1]{0:T(128)} %bitcast.1.here_ref, bf16[1024,256]{1,0:T(8,128)(2,1)S(1)} %maximum_select_fusion.own_ref, bf16[1024,256]{1,0:T(8,128)(2,1)S(1)} %collective-permute-done.1.other_ref, bf16[128,1024]{1,0:T(8,128)(2,1)S(1)} %copy-done.1, ...), custom_call_target="tpu_custom_call", output_to_operand_aliasing={{}: (7, {})} | custom-call | flops 1073741824 | bytes 4194304 | tf_op jit(solution)/shard_map/pallas_call | solution.py:109
  71.7 2.0 %collective-permute-start.20 = (bf16[128,1024]{1,0:T(8,128)(2,1)}, bf16[128,1024]{1,0:T(8,128)(2,1)S(1)}, u32[]{:S(2)}, u32[]{:S(2)}) collective-permute-start(bf16[128,1024]{1,0:T(8,128)(2,1)} %collective-permute-done.11.refs_2_), channel_id=1, source_target_pairs={{0,24},{8,16},{16,8},{24,0},{1,25},{9,17},{17,9},{25,1},{2,26},{10... | collective-permute-start | bytes 786440 | tf_op jit(solution)/shard_map/ppermute | solution.py:55
  73.7 2.3 %shard_map.31.refs_4_ = f32[4,512,256]{2,1,0:T(8,128)S(1)} custom-call(s32[1]{0:T(128)} %bitcast.1.here_ref, bf16[1024,256]{1,0:T(8,128)(2,1)S(1)} %maximum_select_fusion.own_ref, bf16[1024,256]{1,0:T(8,128)(2,1)S(1)} %collective-permute-done.1.other_ref, bf16[128,1024]{1,0:T(8,128)(2,1)} %collective-permute-done.23.refs_0_, ...), custom_call_target="tpu_custom_call", output_to_operand_aliasing={{}: (7, {})} | custom-call | flops 1073741824 | bytes 4194304 | tf_op jit(solution)/shard_map/pallas_call | solution.py:109
  76.1 1.4 %collective-permute-start.6 = (bf16[128,1024]{1,0:T(8,128)(2,1)S(1)}, bf16[128,1024]{1,0:T(8,128)(2,1)S(1)}, u32[]{:S(2)}, u32[]{:S(2)}) collective-permute-start(bf16[128,1024]{1,0:T(8,128)(2,1)S(1)} %collective-permute-done.5.refs_0_), channel_id=1, source_target_pairs={{0,8},{8,0},{16,24},{24,16},{1,9},{9,1},{17,25},{25,17},{2,10},{10... | collective-permute-start | bytes 786440 | tf_op jit(solution)/shard_map/ppermute | solution.py:55
  79.9 2.3 %shard_map.32.refs_4_ = f32[4,512,256]{2,1,0:T(8,128)S(1)} custom-call(s32[1]{0:T(128)} %bitcast.1.here_ref, bf16[1024,256]{1,0:T(8,128)(2,1)S(1)} %maximum_select_fusion.own_ref, bf16[1024,256]{1,0:T(8,128)(2,1)S(1)} %collective-permute-done.1.other_ref, bf16[128,1024]{1,0:T(8,128)(2,1)S(1)} %collective-permute-done.25.refs_0_, ...), custom_call_target="tpu_custom_call", output_to_operand_aliasing={{}: (7, {})} | custom-call | flops 1073741824 | bytes 4194304 | tf_op jit(solution)/shard_map/pallas_call | solution.py:109
  82.2 2.6 %shard_map.33.refs_6_ = f32[4,512,256]{2,1,0:T(8,128)S(1)} custom-call(s32[1]{0:T(128)} %bitcast.1.here_ref, bf16[1024,256]{1,0:T(8,128)(2,1)S(1)} %maximum_select_fusion.own_ref, bf16[1024,256]{1,0:T(8,128)(2,1)S(1)} %collective-permute-done.1.other_ref, bf16[128,1024]{1,0:T(8,128)(2,1)} %collective-permute-done.21.refs_0_, ...), custom_call_target="tpu_custom_call", output_to_operand_aliasing={{}: (7, {})} | custom-call | flops 1073741824 | bytes 4194304 | tf_op jit(solution)/shard_map/pallas_call | solution.py:109
  84.8 3.0 %shard_map.34.refs_4_ = f32[4,512,256]{2,1,0:T(8,128)S(1)} custom-call(s32[1]{0:T(128)} %bitcast.1.here_ref, bf16[1024,256]{1,0:T(8,128)(2,1)S(1)} %maximum_select_fusion.own_ref, bf16[1024,256]{1,0:T(8,128)(2,1)S(1)} %collective-permute-done.1.other_ref, bf16[128,1024]{1,0:T(8,128)(2,1)S(1)} %collective-permute-done.12.refs_0_, ...), custom_call_target="tpu_custom_call", output_to_operand_aliasing={{}: (9, {})} | custom-call | flops 1610612736 | bytes 4194304 | tf_op jit(solution)/shard_map/pallas_call | solution.py:109
  89.7 1.4 %collective-permute-done.34 = f32[4,128,256]{2,1,0:T(8,128)S(1)} collective-permute-done((f32[4,128,256]{2,1,0:T(8,128)S(1)}, f32[4,128,256]{2,1,0:T(8,128)S(1)}, u32[]{:S(2)}, u32[]{:S(2)}) %collective-permute-start.34) | collective-permute-done | bytes 524320 | tf_op jit(solution)/shard_map/ppermute | solution.py:163
  91.2 1.6 %collective-permute-start.35 = (bf16[2,128,256]{2,1,0:T(8,128)(2,1)S(1)}, bf16[2,128,256]{2,1,0:T(8,128)(2,1)S(1)}, u32[]{:S(2)}, u32[]{:S(2)}) collective-permute-start(bf16[2,128,256]{2,1,0:T(8,128)(2,1)S(1)} %get-tuple-element.26), channel_id=1, source_target_pairs={{0,2},{2,0},{1,3},{3,1},{4,6},{6,4},{5,7},{7,5},{8,10},{10,8},{9,1... | collective-permute-start | bytes 393224 | tf_op jit(solution)/shard_map/ppermute | solution.py:166
  92.9 2.2 %collective-permute-start.36 = (bf16[2,128,256]{2,1,0:T(8,128)(2,1)S(1)}, bf16[2,128,256]{2,1,0:T(8,128)(2,1)S(1)}, u32[]{:S(2)}, u32[]{:S(2)}) collective-permute-start(bf16[2,128,256]{2,1,0:T(8,128)(2,1)S(1)} %get-tuple-element.25), channel_id=1, source_target_pairs={{0,3},{3,0},{1,2},{2,1},{4,7},{7,4},{5,6},{6,5},{8,11},{11,8},{9,1... | collective-permute-start | bytes 393224 | tf_op jit(solution)/shard_map/ppermute | solution.py:169
  95.1 1.7 %collective-permute-done.35 = bf16[2,128,256]{2,1,0:T(8,128)(2,1)S(1)} collective-permute-done((bf16[2,128,256]{2,1,0:T(8,128)(2,1)S(1)}, bf16[2,128,256]{2,1,0:T(8,128)(2,1)S(1)}, u32[]{:S(2)}, u32[]{:S(2)}) %collective-permute-start.35) | collective-permute-done | bytes 131104 | tf_op jit(solution)/shard_map/ppermute | solution.py:166
  96.9 2.5 %collective-permute-done.36 = bf16[2,128,256]{2,1,0:T(8,128)(2,1)S(1)} collective-permute-done((bf16[2,128,256]{2,1,0:T(8,128)(2,1)S(1)}, bf16[2,128,256]{2,1,0:T(8,128)(2,1)S(1)}, u32[]{:S(2)}, u32[]{:S(2)}) %collective-permute-start.36) | collective-permute-done | bytes 131104 | tf_op jit(solution)/shard_map/ppermute | solution.py:169
  99.4 2.3 %collective-permute-start.37 = (bf16[128,256]{1,0:T(8,128)(2,1)S(1)}, bf16[128,256]{1,0:T(8,128)(2,1)S(1)}, u32[]{:S(2)}, u32[]{:S(2)}) collective-permute-start(bf16[128,256]{1,0:T(8,128)(2,1)S(1)} %get-tuple-element.22), channel_id=1, source_target_pairs={{0,3},{3,0},{1,2},{2,1},{4,7},{7,4},{5,6},{6,5},{8,11},{11,8},{9,1... | collective-permute-start | bytes 196616 | tf_op jit(solution)/shard_map/ppermute | solution.py:169
  101.7 3.3 %collective-permute-done.37.a_far_ref = bf16[128,256]{1,0:T(8,128)(2,1)S(1)} collective-permute-done((bf16[128,256]{1,0:T(8,128)(2,1)S(1)}, bf16[128,256]{1,0:T(8,128)(2,1)S(1)}, u32[]{:S(2)}, u32[]{:S(2)}) %collective-permute-start.37) | collective-permute-done | bytes 65568 | tf_op jit(solution)/shard_map/ppermute | solution.py:169
  (87 shorter events, 27.6 us)
Async XLA Ops:
  2.3 8.8 %collective-permute-start.1 = (bf16[1024,256]{1,0:T(8,128)(2,1)S(1)}, bf16[1024,256]{1,0:T(8,128)(2,1)S(1)}, u32[]{:S(2)}, u32[]{:S(2)}) collective-permute-start(bf16[1024,256]{1,0:T(8,128)(2,1)S(1)} %maximum_select_fusion.own_ref), channel_id=1, source_target_pairs={{0,4},{4,0},{1,5},{5,1},{2,6},{6,2},{3,7},{7,3},{8,12},{12,8},{9,1... | collective-permute-start | bytes 1572872 | tf_op jit(solution)/shard_map/ppermute | solution.py:163
  2.4 8.7 %collective-permute-start = (bf16[128,1024]{1,0:T(8,128)(2,1)S(1)}, bf16[128,1024]{1,0:T(8,128)(2,1)S(1)}, u32[]{:S(2)}, u32[]{:S(2)}) collective-permute-start(bf16[128,1024]{1,0:T(8,128)(2,1)S(1)} %bitcast.15), channel_id=1, source_target_pairs={{0,8},{8,10},{10,2},{2,0},{16,24},{24,26},{26,18},{18,16},{1,9},{9... | collective-permute-start | bytes 786440 | tf_op jit(solution)/shard_map/ppermute | solution.py:176
  11.1 10.3 %collective-permute-start.28 = (bf16[128,1024]{1,0:T(8,128)(2,1)S(1)}, bf16[128,1024]{1,0:T(8,128)(2,1)S(1)}, u32[]{:S(2)}, u32[]{:S(2)}) collective-permute-start(bf16[128,1024]{1,0:T(8,128)(2,1)S(1)} %collective-permute-done.refs_1_), channel_id=1, source_target_pairs={{0,8},{8,0},{16,24},{24,16},{1,9},{9,1},{17,25},{25,17},{2,10},{10... | collective-permute-start | bytes 786440 | tf_op jit(solution)/shard_map/ppermute | solution.py:55
  12.6 9.9 %collective-permute-start.8 = (bf16[128,1024]{1,0:T(8,128)(2,1)S(1)}, bf16[128,1024]{1,0:T(8,128)(2,1)S(1)}, u32[]{:S(2)}, u32[]{:S(2)}) collective-permute-start(bf16[128,1024]{1,0:T(8,128)(2,1)S(1)} %collective-permute-done.refs_1_), channel_id=1, source_target_pairs={{0,224},{32,64},{64,32},{96,128},{128,96},{160,192},{192,160},{224... | collective-permute-start | bytes 786440 | tf_op jit(solution)/shard_map/ppermute | solution.py:55
  14.5 10.3 %collective-permute-start.2 = (bf16[128,1024]{1,0:T(8,128)(2,1)S(1)}, bf16[128,1024]{1,0:T(8,128)(2,1)S(1)}, u32[]{:S(2)}, u32[]{:S(2)}) collective-permute-start(bf16[128,1024]{1,0:T(8,128)(2,1)S(1)} %collective-permute-done.refs_1_), channel_id=1, source_target_pairs={{0,32},{32,0},{64,96},{96,64},{128,160},{160,128},{192,224},{224,1... | collective-permute-start | bytes 786440 | tf_op jit(solution)/shard_map/ppermute | solution.py:55
  18.6 10.4 %collective-permute-start.16 = (bf16[128,1024]{1,0:T(8,128)(2,1)S(1)}, bf16[128,1024]{1,0:T(8,128)(2,1)S(1)}, u32[]{:S(2)}, u32[]{:S(2)}) collective-permute-start(bf16[128,1024]{1,0:T(8,128)(2,1)S(1)} %collective-permute-done.refs_1_), channel_id=1, source_target_pairs={{0,24},{8,16},{16,8},{24,0},{1,25},{9,17},{17,9},{25,1},{2,26},{10... | collective-permute-start | bytes 786440 | tf_op jit(solution)/shard_map/ppermute | solution.py:55
  21.4 10.9 %collective-permute-start.29 = (bf16[128,1024]{1,0:T(8,128)(2,1)S(1)}, bf16[128,1024]{1,0:T(8,128)(2,1)S(1)}, u32[]{:S(2)}, u32[]{:S(2)}) collective-permute-start(bf16[128,1024]{1,0:T(8,128)(2,1)S(1)} %collective-permute-done.28.refs_0_), channel_id=1, source_target_pairs={{0,24},{8,16},{16,8},{24,0},{1,25},{9,17},{17,9},{25,1},{2,26},{10... | collective-permute-start | bytes 786440 | tf_op jit(solution)/shard_map/ppermute | solution.py:55
  22.5 10.8 %collective-permute-start.32 = (bf16[128,1024]{1,0:T(8,128)(2,1)S(1)}, bf16[128,1024]{1,0:T(8,128)(2,1)S(1)}, u32[]{:S(2)}, u32[]{:S(2)}) collective-permute-start(bf16[128,1024]{1,0:T(8,128)(2,1)S(1)} %collective-permute-done.8.refs_1_), channel_id=1, source_target_pairs={{0,8},{8,0},{16,24},{24,16},{1,9},{9,1},{17,25},{25,17},{2,10},{10... | collective-permute-start | bytes 786440 | tf_op jit(solution)/shard_map/ppermute | solution.py:55
  22.5 12.9 %collective-permute-start.9 = (bf16[128,1024]{1,0:T(8,128)(2,1)S(1)}, bf16[128,1024]{1,0:T(8,128)(2,1)S(1)}, u32[]{:S(2)}, u32[]{:S(2)}) collective-permute-start(bf16[128,1024]{1,0:T(8,128)(2,1)S(1)} %collective-permute-done.8.refs_1_), channel_id=1, source_target_pairs={{0,32},{32,0},{64,96},{96,64},{128,160},{160,128},{192,224},{224,1... | collective-permute-start | bytes 786440 | tf_op jit(solution)/shard_map/ppermute | solution.py:55
  24.9 10.6 %collective-permute-start.3 = (bf16[128,1024]{1,0:T(8,128)(2,1)S(1)}, bf16[128,1024]{1,0:T(8,128)(2,1)S(1)}, u32[]{:S(2)}, u32[]{:S(2)}) collective-permute-start(bf16[128,1024]{1,0:T(8,128)(2,1)S(1)} %collective-permute-done.2.refs_1_), channel_id=1, source_target_pairs={{0,224},{32,64},{64,32},{96,128},{128,96},{160,192},{192,160},{224... | collective-permute-start | bytes 786440 | tf_op jit(solution)/shard_map/ppermute | solution.py:55
  29.0 8.5 %collective-permute-start.31 = (bf16[128,1024]{1,0:T(8,128)(2,1)S(1)}, bf16[128,1024]{1,0:T(8,128)(2,1)S(1)}, u32[]{:S(2)}, u32[]{:S(2)}) collective-permute-start(bf16[128,1024]{1,0:T(8,128)(2,1)S(1)} %collective-permute-done.28.refs_0_), channel_id=1, source_target_pairs={{0,32},{32,0},{64,96},{96,64},{128,160},{160,128},{192,224},{224,1... | collective-permute-start | bytes 786440 | tf_op jit(solution)/shard_map/ppermute | solution.py:55
  33.3 9.0 %collective-permute-start.25 = (bf16[128,1024]{1,0:T(8,128)(2,1)S(1)}, bf16[128,1024]{1,0:T(8,128)(2,1)S(1)}, u32[]{:S(2)}, u32[]{:S(2)}) collective-permute-start(bf16[128,1024]{1,0:T(8,128)(2,1)S(1)} %collective-permute-done.2.refs_1_), channel_id=1, source_target_pairs={{0,24},{8,16},{16,8},{24,0},{1,25},{9,17},{17,9},{25,1},{2,26},{10... | collective-permute-start | bytes 786440 | tf_op jit(solution)/shard_map/ppermute | solution.py:55
  35.4 9.3 %collective-permute-start.10 = (bf16[128,1024]{1,0:T(8,128)(2,1)S(1)}, bf16[128,1024]{1,0:T(8,128)(2,1)}, u32[]{:S(2)}, u32[]{:S(2)}) collective-permute-start(bf16[128,1024]{1,0:T(8,128)(2,1)S(1)} %collective-permute-done.9.refs_3_), channel_id=1, source_target_pairs={{0,8},{8,0},{16,24},{24,16},{1,9},{9,1},{17,25},{25,17},{2,10},{10... | collective-permute-start | bytes 786440 | tf_op jit(solution)/shard_map/ppermute | solution.py:55
  35.4 14.0 %collective-permute-start.23 = (bf16[128,1024]{1,0:T(8,128)(2,1)S(1)}, bf16[128,1024]{1,0:T(8,128)(2,1)}, u32[]{:S(2)}, u32[]{:S(2)}) collective-permute-start(bf16[128,1024]{1,0:T(8,128)(2,1)S(1)} %collective-permute-done.3.refs_1_), channel_id=1, source_target_pairs={{0,8},{8,0},{16,24},{24,16},{1,9},{9,1},{17,25},{25,17},{2,10},{10... | collective-permute-start | bytes 786440 | tf_op jit(solution)/shard_map/ppermute | solution.py:55
  38.2 13.2 %collective-permute-start.30 = (bf16[128,1024]{1,0:T(8,128)(2,1)S(1)}, bf16[128,1024]{1,0:T(8,128)(2,1)S(1)}, u32[]{:S(2)}, u32[]{:S(2)}) collective-permute-start(bf16[128,1024]{1,0:T(8,128)(2,1)S(1)} %collective-permute-done.29.refs_3_), channel_id=1, source_target_pairs={{0,224},{32,64},{64,32},{96,128},{128,96},{160,192},{192,160},{224... | collective-permute-start | bytes 786440 | tf_op jit(solution)/shard_map/ppermute | solution.py:55
  39.9 13.3 %collective-permute-start.21 = (bf16[128,1024]{1,0:T(8,128)(2,1)S(1)}, bf16[128,1024]{1,0:T(8,128)(2,1)}, u32[]{:S(2)}, u32[]{:S(2)}) collective-permute-start(bf16[128,1024]{1,0:T(8,128)(2,1)S(1)} %collective-permute-done.3.refs_1_), channel_id=1, source_target_pairs={{0,24},{8,16},{16,8},{24,0},{1,25},{9,17},{17,9},{25,1},{2,26},{10... | collective-permute-start | bytes 786440 | tf_op jit(solution)/shard_map/ppermute | solution.py:55
  42.4 10.8 %collective-permute-start.18 = (bf16[128,1024]{1,0:T(8,128)(2,1)S(1)}, bf16[128,1024]{1,0:T(8,128)(2,1)S(1)}, u32[]{:S(2)}, u32[]{:S(2)}) collective-permute-start(bf16[128,1024]{1,0:T(8,128)(2,1)S(1)} %collective-permute-done.17.refs_2_), channel_id=1, source_target_pairs={{0,32},{32,0},{64,96},{96,64},{128,160},{160,128},{192,224},{224,1... | collective-permute-start | bytes 786440 | tf_op jit(solution)/shard_map/ppermute | solution.py:55
  44.7 9.7 %collective-permute-start.26 = (bf16[128,1024]{1,0:T(8,128)(2,1)S(1)}, bf16[128,1024]{1,0:T(8,128)(2,1)S(1)}, u32[]{:S(2)}, u32[]{:S(2)}) collective-permute-start(bf16[128,1024]{1,0:T(8,128)(2,1)S(1)} %collective-permute-done.25.refs_0_), channel_id=1, source_target_pairs={{0,8},{8,0},{16,24},{24,16},{1,9},{9,1},{17,25},{25,17},{2,10},{10... | collective-permute-start | bytes 786440 | tf_op jit(solution)/shard_map/ppermute | solution.py:55
  49.5 9.1 %collective-permute-start.4 = (bf16[128,1024]{1,0:T(8,128)(2,1)S(1)}, bf16[128,1024]{1,0:T(8,128)(2,1)}, u32[]{:S(2)}, u32[]{:S(2)}) collective-permute-start(bf16[128,1024]{1,0:T(8,128)(2,1)S(1)} %collective-permute-done.3.refs_1_), channel_id=1, source_target_pairs={{0,32},{32,0},{64,96},{96,64},{128,160},{160,128},{192,224},{224,1... | collective-permute-start | bytes 786440 | tf_op jit(solution)/shard_map/ppermute | solution.py:55
  52.0 10.4 %collective-permute-start.27 = (bf16[128,1024]{1,0:T(8,128)(2,1)}, bf16[128,1024]{1,0:T(8,128)(2,1)}, u32[]{:S(2)}, u32[]{:S(2)}) collective-permute-start(bf16[128,1024]{1,0:T(8,128)(2,1)} %collective-permute-done.10.refs_2_), channel_id=1, source_target_pairs={{0,24},{8,16},{16,8},{24,0},{1,25},{9,17},{17,9},{25,1},{2,26},{10... | collective-permute-start | bytes 786440 | tf_op jit(solution)/shard_map/ppermute | solution.py:55
  53.2 10.4 %collective-permute-start.22 = (bf16[128,1024]{1,0:T(8,128)(2,1)}, bf16[128,1024]{1,0:T(8,128)(2,1)}, u32[]{:S(2)}, u32[]{:S(2)}) collective-permute-start(bf16[128,1024]{1,0:T(8,128)(2,1)} %collective-permute-done.21.refs_0_), channel_id=1, source_target_pairs={{0,8},{8,0},{16,24},{24,16},{1,9},{9,1},{17,25},{25,17},{2,10},{10... | collective-permute-start | bytes 786440 | tf_op jit(solution)/shard_map/ppermute | solution.py:55
  53.2 11.4 %collective-permute-start.11 = (bf16[128,1024]{1,0:T(8,128)(2,1)}, bf16[128,1024]{1,0:T(8,128)(2,1)}, u32[]{:S(2)}, u32[]{:S(2)}) collective-permute-start(bf16[128,1024]{1,0:T(8,128)(2,1)} %collective-permute-done.10.refs_2_), channel_id=1, source_target_pairs={{0,224},{32,64},{64,32},{96,128},{128,96},{160,192},{192,160},{224... | collective-permute-start | bytes 786440 | tf_op jit(solution)/shard_map/ppermute | solution.py:55
  55.1 16.5 %collective-permute-start.24 = (bf16[128,1024]{1,0:T(8,128)(2,1)}, bf16[128,1024]{1,0:T(8,128)(2,1)}, u32[]{:S(2)}, u32[]{:S(2)}) collective-permute-start(bf16[128,1024]{1,0:T(8,128)(2,1)} %collective-permute-done.23.refs_0_), channel_id=1, source_target_pairs={{0,32},{32,0},{64,96},{96,64},{128,160},{160,128},{192,224},{224,1... | collective-permute-start | bytes 786440 | tf_op jit(solution)/shard_map/ppermute | solution.py:55
  58.6 13.1 %collective-permute-start.14 = (bf16[128,1024]{1,0:T(8,128)(2,1)}, bf16[128,1024]{1,0:T(8,128)(2,1)}, u32[]{:S(2)}, u32[]{:S(2)}) collective-permute-start(bf16[128,1024]{1,0:T(8,128)(2,1)} %collective-permute-done.4.refs_3_), channel_id=1, source_target_pairs={{0,224},{32,64},{64,32},{96,128},{128,96},{160,192},{192,160},{224... | collective-permute-start | bytes 786440 | tf_op jit(solution)/shard_map/ppermute | solution.py:55
  62.4 13.6 %collective-permute-start.5 = (bf16[128,1024]{1,0:T(8,128)(2,1)}, bf16[128,1024]{1,0:T(8,128)(2,1)S(1)}, u32[]{:S(2)}, u32[]{:S(2)}) collective-permute-start(bf16[128,1024]{1,0:T(8,128)(2,1)} %collective-permute-done.4.refs_3_), channel_id=1, source_target_pairs={{0,24},{8,16},{16,8},{24,0},{1,25},{9,17},{17,9},{25,1},{2,26},{10... | collective-permute-start | bytes 786440 | tf_op jit(solution)/shard_map/ppermute | solution.py:55
  63.6 13.9 %collective-permute-start.19 = (bf16[128,1024]{1,0:T(8,128)(2,1)S(1)}, bf16[128,1024]{1,0:T(8,128)(2,1)S(1)}, u32[]{:S(2)}, u32[]{:S(2)}) collective-permute-start(bf16[128,1024]{1,0:T(8,128)(2,1)S(1)} %copy-done.3), channel_id=1, source_target_pairs={{0,224},{32,64},{64,32},{96,128},{128,96},{160,192},{192,160},{224... | collective-permute-start | bytes 786440 | tf_op jit(solution)/shard_map/ppermute | solution.py:55
  64.6 13.9 %collective-permute-start.12 = (bf16[128,1024]{1,0:T(8,128)(2,1)}, bf16[128,1024]{1,0:T(8,128)(2,1)S(1)}, u32[]{:S(2)}, u32[]{:S(2)}) collective-permute-start(bf16[128,1024]{1,0:T(8,128)(2,1)} %collective-permute-done.11.refs_2_), channel_id=1, source_target_pairs={{0,32},{32,0},{64,96},{96,64},{128,160},{160,128},{192,224},{224,1... | collective-permute-start | bytes 786440 | tf_op jit(solution)/shard_map/ppermute | solution.py:55
  71.6 13.2 %collective-permute-start.15 = (bf16[128,1024]{1,0:T(8,128)(2,1)}, bf16[128,1024]{1,0:T(8,128)(2,1)S(1)}, u32[]{:S(2)}, u32[]{:S(2)}) collective-permute-start(bf16[128,1024]{1,0:T(8,128)(2,1)} %collective-permute-done.11.refs_2_), channel_id=1, source_target_pairs={{0,8},{8,0},{16,24},{24,16},{1,9},{9,1},{17,25},{25,17},{2,10},{10... | collective-permute-start | bytes 786440 | tf_op jit(solution)/shard_map/ppermute | solution.py:55
  71.7 13.1 %collective-permute-start.20 = (bf16[128,1024]{1,0:T(8,128)(2,1)}, bf16[128,1024]{1,0:T(8,128)(2,1)S(1)}, u32[]{:S(2)}, u32[]{:S(2)}) collective-permute-start(bf16[128,1024]{1,0:T(8,128)(2,1)} %collective-permute-done.11.refs_2_), channel_id=1, source_target_pairs={{0,24},{8,16},{16,8},{24,0},{1,25},{9,17},{17,9},{25,1},{2,26},{10... | collective-permute-start | bytes 786440 | tf_op jit(solution)/shard_map/ppermute | solution.py:55
  76.1 11.7 %collective-permute-start.6 = (bf16[128,1024]{1,0:T(8,128)(2,1)S(1)}, bf16[128,1024]{1,0:T(8,128)(2,1)S(1)}, u32[]{:S(2)}, u32[]{:S(2)}) collective-permute-start(bf16[128,1024]{1,0:T(8,128)(2,1)S(1)} %collective-permute-done.5.refs_0_), channel_id=1, source_target_pairs={{0,8},{8,0},{16,24},{24,16},{1,9},{9,1},{17,25},{25,17},{2,10},{10... | collective-permute-start | bytes 786440 | tf_op jit(solution)/shard_map/ppermute | solution.py:55
  77.5 10.3 %collective-permute-start.7 = (bf16[128,1024]{1,0:T(8,128)(2,1)S(1)}, bf16[128,1024]{1,0:T(8,128)(2,1)S(1)}, u32[]{:S(2)}, u32[]{:S(2)}) collective-permute-start(bf16[128,1024]{1,0:T(8,128)(2,1)S(1)} %collective-permute-done.5.refs_0_), channel_id=1, source_target_pairs={{0,224},{32,64},{64,32},{96,128},{128,96},{160,192},{192,160},{224... | collective-permute-start | bytes 786440 | tf_op jit(solution)/shard_map/ppermute | solution.py:55
  78.5 9.3 %collective-permute-start.13 = (bf16[128,1024]{1,0:T(8,128)(2,1)S(1)}, bf16[128,1024]{1,0:T(8,128)(2,1)S(1)}, u32[]{:S(2)}, u32[]{:S(2)}) collective-permute-start(bf16[128,1024]{1,0:T(8,128)(2,1)S(1)} %collective-permute-done.12.refs_0_), channel_id=1, source_target_pairs={{0,24},{8,16},{16,8},{24,0},{1,25},{9,17},{17,9},{25,1},{2,26},{10... | collective-permute-start | bytes 786440 | tf_op jit(solution)/shard_map/ppermute | solution.py:55
  (20 other events, 74.1 us)
